TPU v7x, 32 devices: a whole 2x2x4 slice. The times are simulated.
32 devices in a mesh: row: 4 (over x, core), col: 8 (over z, y).
Axes of the slice: x: 2, y: 2, z: 4, core: 2. Of those that a mesh axis runs over, the one named last changes fastest.
Arguments:
- rhs: float32 [32768, 512], P('col', 'row'), may hold values from -6 to 6
- factors: bfloat16 [32768, 2048], P('col', 'row'), may hold values from -0.15625 to 0.15625
- diag_inv: float32 [4, 512, 512], replicated, may hold values from -2 to 2, as said below
Outputs:
- solution: float32 [32768, 512], P('col', 'row')
Inputs may be any that keep to these rules, and one draw needn't show every extreme that they name: `diag_inv`: entries off the diagonal of each block lie within 2 / sqrt(512) in magnitude; diagonal entries lie in 0.5 to 2.
All inputs are finite; a program needn't handle non-finite values.
Results may differ from a plain program's by a relative error of at most 0.0038.
Values may be sent and summed in bfloat16 or wider, within the bound.
A program may use at most 128 MiB of HBM per device.

v0:
```python
import jax
import jax.numpy as jnp
from jax import lax
from jax.sharding import PartitionSpec as P


def body(rhs, factors, diag_inv):
    rows_dev = rhs.shape[0]
    steps = diag_inv.shape[0]
    block = diag_inv.shape[1]
    col_count = lax.axis_size("col")
    block_span = rows_dev * col_count // steps
    my_index = lax.axis_index("col")
    global_rows = my_index * rows_dev + jnp.arange(rows_dev)
    index = jnp.arange(block)
    strict_lower = index[:, None] > index[None, :]
    eye = jnp.eye(block, dtype=jnp.float32)
    panel_rows = lax.all_gather(factors, "row", axis=1, tiled=True)

    def solve_block(matrix, work, step):
        owner_index = step * col_count // steps
        owner = my_index == owner_index
        product = jnp.dot(
            matrix,
            work[:block],
            precision=lax.Precision.HIGHEST,
            preferred_element_type=jnp.float32,
        )
        solved = lax.psum(jnp.where(owner, product, jnp.float32(0.0)), "col")
        return (solved, owner)

    def apply_update(work, solved, owner, columns, row_mask):
        product = jnp.dot(columns, solved.astype(jnp.bfloat16), preferred_element_type=jnp.float32)
        updated = jnp.where(row_mask[:, None], work - product, work)
        leading = jnp.where(owner, solved, updated[:block])
        return jnp.concatenate([leading, updated[block:]], axis=0)

    work = rhs
    kept_columns = []
    for step in range(steps):
        lower_inv = jnp.where(strict_lower, diag_inv[step], jnp.float32(0.0)) + eye
        solved, owner = solve_block(lower_inv, work, step)
        columns = panel_rows[:, step * block : (step + 1) * block]
        kept_columns.append(columns)
        row_mask = global_rows >= step * block_span + block
        work = apply_update(work, solved, owner, columns, row_mask)
    for step in reversed(range(steps)):
        upper_inv = jnp.triu(diag_inv[step])
        solved, owner = solve_block(upper_inv, work, step)
        row_mask = global_rows < step * block_span
        work = apply_update(work, solved, owner, kept_columns[step], row_mask)
    return work


def solution(mesh):
    placed = (P("col", "row"), P("col", "row"), P())
    return jax.shard_map(
        body, mesh=mesh, in_specs=placed, out_specs=P("col", "row"), check_vma=False
    )
```

profile of v0, /device:TPU:0, one launch (start us, length us, event | category | flops | bytes accessed | tf_op | source)
XLA Modules:
  0.0 677.5 jit_solution(9635209791874704113)
XLA Ops:
  7.4 0.0 all-reduce.9.cloned.1.call-start
  7.4 3.0 convolution_select_fusion.7
  10.3 0.0 all-reduce.9.cloned.1.call-update
  10.3 0.0 all-gather.2.cloned.1.call-start
  10.4 0.5 all-gather.2.cloned.1.call-update
  10.9 0.0 all-reduce.11.cloned.1.call-start
  11.0 74.3 %all-reduce.9.cloned.1.call-done = f32[512,128]{1,0:T(8,128)} async-done(((f32[512,128]{1,0:T(8,128)}), f32[512,128]{1,0:T(8,128)}) %all-reduce.9.cloned.1.call-update) | async-done | bytes 262160 | tf_op jit(solution)/shard_map/psum | solution.py:29
  85.3 0.0 copy-start
  85.3 35.6 %all-gather.2.cloned.1.call-done = bf16[4096,2048]{1,0:T(8,128)(2,1)} async-done(((bf16[4096,512]{1,0:T(8,128)(2,1)}), bf16[4096,2048]{1,0:T(8,128)(2,1)}) %all-gather.2.cloned.1.call-update) | async-done | bytes 16777232 | tf_op jit(solution)/shard_map/all_gather | solution.py:18
  120.9 3.6 fusion.15
  124.6 0.0 copy-done
  124.6 2.9 convolution_select_fusion.6
  127.5 0.0 all-reduce.11.cloned.1.call-update
  127.5 0.0 all-reduce.13.cloned.1.call-start
  127.6 1.3 slice.106
  129.0 69.8 %all-reduce.11.cloned.1.call-done = f32[512,128]{1,0:T(8,128)} async-done(((f32[512,128]{1,0:T(8,128)}), f32[512,128]{1,0:T(8,128)}) %all-reduce.11.cloned.1.call-update) | async-done | bytes 262160 | tf_op jit(solution)/shard_map/psum | solution.py:29
  198.7 0.0 copy-start.2
  198.8 4.1 fusion.13
  202.9 0.0 copy-done.2
  202.9 2.9 convolution_select_fusion.5
  205.8 0.0 all-reduce.13.cloned.1.call-update
  205.9 0.0 all-reduce.15.cloned.1.call-start
  205.9 1.3 slice.109
  207.3 68.9 %all-reduce.13.cloned.1.call-done = f32[512,128]{1,0:T(8,128)} async-done(((f32[512,128]{1,0:T(8,128)}), f32[512,128]{1,0:T(8,128)}) %all-reduce.13.cloned.1.call-update) | async-done | bytes 262160 | tf_op jit(solution)/shard_map/psum | solution.py:29
  276.2 0.0 copy-start.1
  276.2 4.1 fusion.11
  280.3 0.0 copy-done.1
  280.3 2.9 convolution_select_fusion.4
  283.3 0.0 all-reduce.15.cloned.1.call-update
  283.3 0.0 all-reduce.17.cloned.1.call-start
  283.4 1.3 slice.112
  284.7 69.0 %all-reduce.15.cloned.1.call-done = f32[512,128]{1,0:T(8,128)} async-done(((f32[512,128]{1,0:T(8,128)}), f32[512,128]{1,0:T(8,128)}) %all-reduce.15.cloned.1.call-update) | async-done | bytes 262160 | tf_op jit(solution)/shard_map/psum | solution.py:29
  353.7 4.2 fusion.9
  357.9 0.0 copy-done.4
  358.0 3.0 convolution_select_fusion.3
  360.9 0.0 all-reduce.17.cloned.1.call-update
  361.0 0.0 all-reduce.19.cloned.1.call-start
  361.0 1.3 slice.115
  362.4 69.0 %all-reduce.17.cloned.1.call-done = f32[512,128]{1,0:T(8,128)} async-done(((f32[512,128]{1,0:T(8,128)}), f32[512,128]{1,0:T(8,128)}) %all-reduce.17.cloned.1.call-update) | async-done | bytes 262160 | tf_op jit(solution)/shard_map/psum | solution.py:29
  431.4 4.2 fusion.7
  435.6 0.0 copy-done.5
  435.6 3.0 convolution_select_fusion.2
  438.6 0.0 all-reduce.19.cloned.1.call-update
  438.6 0.2 all-reduce.21.cloned.1.call-start
  438.9 1.3 slice.117
  440.2 68.8 %all-reduce.19.cloned.1.call-done = f32[512,128]{1,0:T(8,128)} async-done(((f32[512,128]{1,0:T(8,128)}), f32[512,128]{1,0:T(8,128)}) %all-reduce.19.cloned.1.call-update) | async-done | bytes 262160 | tf_op jit(solution)/shard_map/psum | solution.py:29
  509.0 4.1 fusion.5
  513.1 0.0 copy-done.6
  513.1 3.0 convolution_select_fusion.1
  516.1 0.0 all-reduce.21.cloned.1.call-update
  516.1 0.0 all-reduce.23.cloned.1.call-start
  516.2 1.3 slice.119
  517.5 68.9 %all-reduce.21.cloned.1.call-done = f32[512,128]{1,0:T(8,128)} async-done(((f32[512,128]{1,0:T(8,128)}), f32[512,128]{1,0:T(8,128)}) %all-reduce.21.cloned.1.call-update) | async-done | bytes 262160 | tf_op jit(solution)/shard_map/psum | solution.py:29
  586.5 4.1 fusion.3
  590.6 0.0 copy-done.7
  590.6 3.0 convolution_select_fusion
  593.6 0.0 all-reduce.23.cloned.1.call-update
  593.7 1.3 slice.121
  595.0 69.1 %all-reduce.23.cloned.1.call-done = f32[512,128]{1,0:T(8,128)} async-done(((f32[512,128]{1,0:T(8,128)}), f32[512,128]{1,0:T(8,128)}) %all-reduce.23.cloned.1.call-update) | async-done | bytes 262160 | tf_op jit(solution)/shard_map/psum | solution.py:29
  664.1 3.6 fusion.1
  667.6 0.0 copy-start.3
  667.6 0.1 slice.123
  667.8 0.8 copy-done.3
  668.6 1.5 pad_maximum_fusion
  (21 shorter events, 0.4 us)
Async XLA Ops:
  7.4 77.9 %all-reduce.9.cloned.1.call-start = ((), (), s32[]{:S(2)}) async-start(), calls=%async_computation | async-start | bytes 524288 | tf_op jit(solution)/shard_map/psum | solution.py:29
  10.3 110.6 %all-gather.2.cloned.1.call-start = ((), (), s32[]{:S(2)}) async-start(), calls=%async_computation.1 | async-start | bytes 20971520 | tf_op jit(solution)/shard_map/all_gather | solution.py:18
  10.9 187.8 %all-reduce.11.cloned.1.call-start = ((), (), s32[]{:S(2)}) async-start(), calls=%async_computation.2 | async-start | bytes 524288 | tf_op jit(solution)/shard_map/psum | solution.py:29
  85.3 39.3 %copy-start = (f32[512,128]{1,0:T(8,128)S(1)}, f32[512,128]{1,0:T(8,128)}, u32[]{:S(2)}) copy-start(f32[512,128]{1,0:T(8,128)} %all-reduce.9.cloned.1.call-done) | copy-start | bytes 786436
  127.5 148.7 %all-reduce.13.cloned.1.call-start = ((), (), s32[]{:S(2)}) async-start(), calls=%async_computation.3 | async-start | bytes 524288 | tf_op jit(solution)/shard_map/psum | solution.py:29
  198.7 4.1 copy-start.2
  205.9 147.8 %all-reduce.15.cloned.1.call-start = ((), (), s32[]{:S(2)}) async-start(), calls=%async_computation.4 | async-start | bytes 524288 | tf_op jit(solution)/shard_map/psum | solution.py:29
  276.2 4.1 copy-start.1
  283.3 148.1 %all-reduce.17.cloned.1.call-start = ((), (), s32[]{:S(2)}) async-start(), calls=%async_computation.5 | async-start | bytes 524288 | tf_op jit(solution)/shard_map/psum | solution.py:29
  353.7 4.2 copy-start.4
  361.0 148.0 %all-reduce.19.cloned.1.call-start = ((), (), s32[]{:S(2)}) async-start(), calls=%async_computation.6 | async-start | bytes 524288 | tf_op jit(solution)/shard_map/psum | solution.py:29
  431.4 4.2 copy-start.5
  438.6 147.8 %all-reduce.21.cloned.1.call-start = ((), (), s32[]{:S(2)}) async-start(), calls=%async_computation.7 | async-start | bytes 524288 | tf_op jit(solution)/shard_map/psum | solution.py:29
  509.0 4.1 copy-start.6
  516.1 147.9 %all-reduce.23.cloned.1.call-start = ((), (), s32[]{:S(2)}) async-start(), calls=%async_computation.8 | async-start | bytes 524288 | tf_op jit(solution)/shard_map/psum | solution.py:29
  586.5 4.1 copy-start.7
  667.6 1.0 copy-start.3
Sparse Core Ops, SparseCore 0:
  11.5 73.7 all-reduce.8
  127.7 71.0 all-reduce.10
  206.0 70.1 all-reduce.12
  283.4 70.2 all-reduce.14
  361.1 70.2 all-reduce.16
  438.8 70.1 all-reduce.18
  516.2 70.1 all-reduce.20
  593.8 70.2 all-reduce.22
Sparse Core Ops, SparseCore 1:
  12.4 108.5 all-gather.1
where the time goes:
time: 678 us
  waiting for transfers between devices  594 us (88%)
  matrix products  55.6 us (8%)
  between operations  15.2 us (2%)
  local copies, waits for them, and re-layouts  10.4 us (2%)
    psum x8, waiting for transfers between devices, solve_block(): solved = lax.psum(jnp.where(owner, product, jnp.float32(0.0)), 'col')  558 us
    all_gather x1, waiting for transfers between devices, body(): panel_rows = lax.all_gather(factors, 'row', axis=1, tiled=True)  35.6 us
    dot_general x8, matrix products, apply_update(): jnp.dot(columns, solved.astype(jnp.bfloat16), preferred_element_type=jnp....  32 us
    dot_general x8, matrix products, solve_block(): jnp.dot(matrix, work[:block], precision=lax.Precision.HIGHEST, preferred_...  23.6 us
  transfers between devices with their start and end apart: 9, of which 9 were waited for; matrix products, arithmetic and copies ran while one was open for 1% of the time, Pallas kernels for 0%

commit v1 on v0

--- a/solution.py
+++ b/solution.py
@@ -26,7 +26,7 @@
             precision=lax.Precision.HIGHEST,
             preferred_element_type=jnp.float32,
         )
-        solved = lax.psum(jnp.where(owner, product, jnp.float32(0.0)), "col")
+        solved = jnp.sum(lax.all_gather(jnp.where(owner, product, jnp.float32(0.0)), "col"), axis=0)
         return (solved, owner)
 
     def apply_update(work, solved, owner, columns, row_mask):

time: 678 us -> 586 us (0.86)
  waiting for transfers between devices: 594 us -> 489 us
  other arithmetic: 1.82 us -> 15.8 us
    psum x8 -> x0, waiting for transfers between devices: 558 us -> none  [solve_block(): solved = lax.psum(jnp.where(owner, product, jnp.float32(0.0)), 'col')]
    all_gather x0 -> x8, waiting for transfers between devices: none -> 384 us  [solve_block(): lax.all_gather(jnp.where(owner, product, jnp.float32(0.0)), 'col')]
    all_gather x1, waiting for transfers between devices: 35.6 us -> 104 us  [body(): panel_rows = lax.all_gather(factors, 'row', axis=1, tiled=True)]
    reduce_sum x0 -> x8, other arithmetic: none -> 14 us  [solve_block(): jnp.sum(lax.all_gather(jnp.where(owner, product, jnp.float32(0.0)), 'col'...]
where the time goes in v1:
time: 586 us; the launch traced here: 585 us
  waiting for transfers between devices  489 us (83%)
  matrix products  55.9 us (10%)
  other arithmetic  15.8 us (3%)
  between operations  13.5 us (2%)
  local copies, waits for them, and re-layouts  10.1 us (2%)
    all_gather x8, waiting for transfers between devices, solve_block(): lax.all_gather(jnp.where(owner, product, jnp.float32(0.0)), 'col')  384 us
    all_gather x1, waiting for transfers between devices, body(): panel_rows = lax.all_gather(factors, 'row', axis=1, tiled=True)  104 us
    dot_general x8, matrix products, apply_update(): jnp.dot(columns, solved.astype(jnp.bfloat16), preferred_element_type=jnp....  30.8 us
    dot_general x8, matrix products, solve_block(): jnp.dot(matrix, work[:block], precision=lax.Precision.HIGHEST, preferred_...  25.1 us
    reduce_sum x8, other arithmetic, solve_block(): jnp.sum(lax.all_gather(jnp.where(owner, product, jnp.float32(0.0)), 'col'...  14 us
  transfers between devices with their start and end apart: 9, of which 9 were waited for; matrix products, arithmetic and copies ran while one was open for 1% of the time, Pallas kernels for 0%

profile of v1, /device:TPU:0, one launch (start us, length us, event | category | flops | bytes accessed | tf_op | source)
XLA Modules:
  0.0 584.6 jit_solution(16530183244064792842)
XLA Ops:
  6.5 3.0 convolution_select_fusion.7
  9.5 0.0 all-gather.20.cloned.1.call-update
  9.5 0.0 all-gather.18.cloned.1.call-start
  9.6 0.7 all-gather.18.cloned.1.call-update
  10.3 0.0 all-gather.22.cloned.1.call-start
  10.3 51.1 %all-gather.20.cloned.1.call-done = f32[4096,128]{1,0:T(8,128)} async-done(((f32[512,128]{1,0:T(8,128)}), f32[4096,128]{1,0:T(8,128)}) %all-gather.20.cloned.1.call-update) | async-done | bytes 2097168 | tf_op jit(solution)/shard_map/all_gather | solution.py:29
  61.5 1.7 reduce_sum.72
  63.2 104.3 %all-gather.18.cloned.1.call-done = bf16[4096,2048]{1,0:T(8,128)(2,1)} async-done(((bf16[4096,512]{1,0:T(8,128)(2,1)}), bf16[4096,2048]{1,0:T(8,128)(2,1)}) %all-gather.18.cloned.1.call-update) | async-done | bytes 16777232 | tf_op jit(solution)/shard_map/all_gather | solution.py:18
  167.5 3.6 fusion.15
  171.1 3.6 convolution_select_fusion.6
  174.8 0.0 all-gather.22.cloned.1.call-update
  174.8 0.0 all-gather.24.cloned.1.call-start
  174.9 49.2 %all-gather.22.cloned.1.call-done = f32[4096,128]{1,0:T(8,128)} async-done(((f32[512,128]{1,0:T(8,128)}), f32[4096,128]{1,0:T(8,128)}) %all-gather.22.cloned.1.call-update) | async-done | bytes 2097168 | tf_op jit(solution)/shard_map/all_gather | solution.py:29
  224.1 1.8 reduce_sum.73
  225.9 0.3 slice-done
  226.2 4.0 fusion.13
  230.2 1.3 copy-done.1
  231.5 2.9 convolution_select_fusion.5
  234.4 0.0 all-gather.24.cloned.1.call-update
  234.5 0.0 all-gather.26.cloned.1.call-start
  234.5 0.0 slice-start.1
  234.5 47.7 %all-gather.24.cloned.1.call-done = f32[4096,128]{1,0:T(8,128)} async-done(((f32[512,128]{1,0:T(8,128)}), f32[4096,128]{1,0:T(8,128)}) %all-gather.24.cloned.1.call-update) | async-done | bytes 2097168 | tf_op jit(solution)/shard_map/all_gather | solution.py:29
  282.2 1.7 reduce_sum.74
  284.0 4.0 fusion.11
  287.9 1.3 copy-done.2
  289.3 2.9 convolution_select_fusion.4
  292.2 0.0 all-gather.26.cloned.1.call-update
  292.2 0.0 all-gather.28.cloned.1.call-start
  292.3 0.0 slice-start.2
  292.3 47.7 %all-gather.26.cloned.1.call-done = f32[4096,128]{1,0:T(8,128)} async-done(((f32[512,128]{1,0:T(8,128)}), f32[4096,128]{1,0:T(8,128)}) %all-gather.26.cloned.1.call-update) | async-done | bytes 2097168 | tf_op jit(solution)/shard_map/all_gather | solution.py:29
  340.0 1.7 reduce_sum.75
  341.7 4.0 fusion.9
  345.7 1.3 copy-done.6
  347.1 3.0 convolution_select_fusion.3
  350.0 0.0 all-gather.28.cloned.1.call-update
  350.1 0.0 all-gather.30.cloned.1.call-start
  350.1 2.9 slice.115
  353.0 44.9 %all-gather.28.cloned.1.call-done = f32[4096,128]{1,0:T(8,128)} async-done(((f32[512,128]{1,0:T(8,128)}), f32[4096,128]{1,0:T(8,128)}) %all-gather.28.cloned.1.call-update) | async-done | bytes 2097168 | tf_op jit(solution)/shard_map/all_gather | solution.py:29
  397.8 1.7 reduce_sum.76
  399.6 3.5 fusion.7
  403.1 3.7 convolution_select_fusion.2
  406.8 0.0 all-gather.30.cloned.1.call-update
  406.9 0.2 all-gather.32.cloned.1.call-start
  407.1 47.5 %all-gather.30.cloned.1.call-done = f32[4096,128]{1,0:T(8,128)} async-done(((f32[512,128]{1,0:T(8,128)}), f32[4096,128]{1,0:T(8,128)}) %all-gather.30.cloned.1.call-update) | async-done | bytes 2097168 | tf_op jit(solution)/shard_map/all_gather | solution.py:29
  454.6 1.8 reduce_sum.77
  456.5 0.3 slice-done.3
  456.8 3.9 fusion.5
  460.7 1.3 copy-done.4
  462.1 3.0 convolution_select_fusion.1
  465.1 0.0 all-gather.32.cloned.1.call-update
  465.1 0.0 all-gather.34.cloned.1.call-start
  465.2 0.0 slice-start.4
  465.2 47.7 %all-gather.32.cloned.1.call-done = f32[4096,128]{1,0:T(8,128)} async-done(((f32[512,128]{1,0:T(8,128)}), f32[4096,128]{1,0:T(8,128)}) %all-gather.32.cloned.1.call-update) | async-done | bytes 2097168 | tf_op jit(solution)/shard_map/all_gather | solution.py:29
  512.9 1.7 reduce_sum.78
  514.6 4.0 fusion.3
  518.6 1.3 copy-done.5
  519.9 3.0 convolution_select_fusion
  522.9 0.0 all-gather.34.cloned.1.call-update
  522.9 0.0 slice-start.5
  523.0 47.7 %all-gather.34.cloned.1.call-done = f32[4096,128]{1,0:T(8,128)} async-done(((f32[512,128]{1,0:T(8,128)}), f32[4096,128]{1,0:T(8,128)}) %all-gather.34.cloned.1.call-update) | async-done | bytes 2097168 | tf_op jit(solution)/shard_map/all_gather | solution.py:29
  570.7 1.7 reduce_sum.79
  572.4 4.0 fusion.1
  576.4 0.1 slice.123
  576.6 1.5 pad_maximum_fusion
  (33 shorter events, 0.4 us)
Async XLA Ops:
  6.5 54.9 %all-gather.20.cloned.1.call-start = ((), (), s32[]{:S(2)}) async-start(), calls=%async_computation.1 | async-start | bytes 2359296 | tf_op jit(solution)/shard_map/all_gather | solution.py:29
  9.5 158.0 %all-gather.18.cloned.1.call-start = ((), (), s32[]{:S(2)}) async-start(), calls=%async_computation | async-start | bytes 20971520 | tf_op jit(solution)/shard_map/all_gather | solution.py:18
  10.3 213.8 %all-gather.22.cloned.1.call-start = ((), (), s32[]{:S(2)}) async-start(), calls=%async_computation.2 | async-start | bytes 2359296 | tf_op jit(solution)/shard_map/all_gather | solution.py:29
  171.1 3.8 copy-start
  174.8 107.4 %all-gather.24.cloned.1.call-start = ((), (), s32[]{:S(2)}) async-start(), calls=%async_computation.3 | async-start | bytes 2359296 | tf_op jit(solution)/shard_map/all_gather | solution.py:29
  224.1 2.1 slice-start
  230.1 1.3 copy-start.1
  234.5 105.5 %all-gather.26.cloned.1.call-start = ((), (), s32[]{:S(2)}) async-start(), calls=%async_computation.4 | async-start | bytes 2359296 | tf_op jit(solution)/shard_map/all_gather | solution.py:29
  234.5 49.4 %slice-start.1 = ((f32[4096,128]{1,0:T(8,128)}), f32[3584,128]{1,0:T(8,128)S(1)}, s32[]{:S(2)}) async-start(f32[4096,128]{1,0:T(8,128)} %copy-done.1), calls=%async_computation.10 | async-start | bytes 3670016 | tf_op jit(solution)/shard_map/slice | solution.py:36
  287.9 1.3 copy-start.2
  292.2 105.6 %all-gather.28.cloned.1.call-start = ((), (), s32[]{:S(2)}) async-start(), calls=%async_computation.5 | async-start | bytes 2359296 | tf_op jit(solution)/shard_map/all_gather | solution.py:29
  292.3 49.4 %slice-start.2 = ((f32[4096,128]{1,0:T(8,128)}), f32[3584,128]{1,0:T(8,128)S(1)}, s32[]{:S(2)}) async-start(f32[4096,128]{1,0:T(8,128)} %copy-done.2), calls=%async_computation.11 | async-start | bytes 3670016 | tf_op jit(solution)/shard_map/slice | solution.py:36
  345.7 1.3 copy-start.6
  350.1 104.6 %all-gather.30.cloned.1.call-start = ((), (), s32[]{:S(2)}) async-start(), calls=%async_computation.6 | async-start | bytes 2359296 | tf_op jit(solution)/shard_map/all_gather | solution.py:29
  403.1 4.0 copy-start.3
  406.9 106.0 %all-gather.32.cloned.1.call-start = ((), (), s32[]{:S(2)}) async-start(), calls=%async_computation.7 | async-start | bytes 2359296 | tf_op jit(solution)/shard_map/all_gather | solution.py:29
  454.6 2.1 slice-start.3
  460.7 1.3 copy-start.4
  465.1 105.6 %all-gather.34.cloned.1.call-start = ((), (), s32[]{:S(2)}) async-start(), calls=%async_computation.8 | async-start | bytes 2359296 | tf_op jit(solution)/shard_map/all_gather | solution.py:29
  465.2 49.4 %slice-start.4 = ((f32[4096,128]{1,0:T(8,128)}), f32[3584,128]{1,0:T(8,128)S(1)}, s32[]{:S(2)}) async-start(f32[4096,128]{1,0:T(8,128)} %copy-done.4), calls=%async_computation.13 | async-start | bytes 3670016 | tf_op jit(solution)/shard_map/slice | solution.py:36
  518.6 1.3 copy-start.5
  522.9 49.5 %slice-start.5 = ((f32[4096,128]{1,0:T(8,128)}), f32[3584,128]{1,0:T(8,128)S(1)}, s32[]{:S(2)}) async-start(f32[4096,128]{1,0:T(8,128)} %copy-done.5), calls=%async_computation.14 | async-start | bytes 3670016 | tf_op jit(solution)/shard_map/slice | solution.py:36
Sparse Core Ops, SparseCore 0:
  9.6 51.7 all-gather.19
  63.0 104.4 all-gather.17
  174.9 49.0 all-gather.21
  234.6 47.6 all-gather.23
  292.4 47.5 all-gather.25
  350.2 47.6 all-gather.27
  407.0 47.6 all-gather.29
  465.2 47.6 all-gather.31
  523.1 47.6 all-gather.33
